TPU v7x, 512 devices: a whole 4x4x16 slice. The times are simulated.
512 devices in a mesh: section: 4 (over x), trial: 128 (over z, y, core).
Axes of the slice: x: 4, y: 4, z: 16, core: 2. Of those that a mesh axis runs over, the one named last changes fastest.
Arguments:
- spike_rates: bfloat16 [512, 256, 256], P(None, 'trial'), may hold values from -6 to 6
- first_preactivation: bfloat16 [1024, 256, 256], P('section', 'trial'), may hold values from -6 to 6
- second_preactivation: bfloat16 [1024, 256, 256], P('section', 'trial'), may hold values from -6 to 6
- output_gradient: bfloat16 [1024, 256, 256], P('section', 'trial'), may hold values from -0.29882812 to 0.29882812
- first_kernel: bfloat16 [3, 1024, 1024], P(None, None, 'section'), may hold values from -0.109375 to 0.109375
- second_kernel: bfloat16 [3, 1024, 1024], P(None, None, 'section'), may hold values from -0.109375 to 0.109375
- session_of: int32 [256], P('trial'), may hold values from 0 to 127, never falling along the last dimension, each value on 1 to 6 neighbouring positions
Outputs:
- readin_grad: bfloat16 [128, 512, 1024], P(None, 'trial', 'section')
Inputs may be any that keep to these rules, and one draw needn't show every extreme that they name: `session_of`: the trials of a session are consecutive; every session has 1 to 6 trials, and one has exactly 6.
All inputs are finite; a program needn't handle non-finite values.
Results may differ from a plain program's by a relative error of at most 0.017.
Values may be sent and summed in bfloat16 or wider, within the bound.
No kernel may reach another device: no remote copies, remote signals or barrier semaphores. Data moves between devices by JAX's collectives and lax.ppermute only.
A program may use at most 64 MiB of HBM per device.

v0:
```python
import math
import jax
import jax.numpy as jnp
from jax import lax
from jax.sharding import PartitionSpec as P

FIRST_DILATION = 32
SECOND_DILATION = 64
MOST = 6


def gelu_slope(preact):
    values = preact.astype(jnp.float32)
    normal_cdf = 0.5 * (1.0 + lax.erf(values * (1.0 / math.sqrt(2.0))))
    density = jnp.exp(-0.5 * values * values) * (1.0 / math.sqrt(2.0 * math.pi))
    return normal_cdf + values * density


def shift_ahead(values, offset):
    padding = [(0, 0)] * (values.ndim - 1) + [(0, offset)]
    return jnp.pad(values[..., offset:], padding)


def tap_sum(weights, flow_grad, spacing):
    running = None
    for kernel_tap in range(3):
        term_tap = lax.dot_general(
            weights[kernel_tap],
            flow_grad,
            (((1,), (0,)), ((), ())),
            preferred_element_type=jnp.float32,
        )
        if kernel_tap > 0:
            term_tap = shift_ahead(term_tap, kernel_tap * spacing)
        running = term_tap if running is None else running + term_tap
    return running


def layer_backprop(upstream, preact, turned, spacing):
    flow_grad = (upstream.astype(jnp.float32) * gelu_slope(preact)).astype(jnp.bfloat16)
    back_sum = tap_sum(turned, lax.all_gather(flow_grad, "section", axis=0, tiled=True), spacing)
    return (upstream.astype(jnp.float32) + back_sum).astype(jnp.bfloat16)


def body(
    spike_rates,
    first_preactivation,
    second_preactivation,
    output_gradient,
    first_kernel,
    second_kernel,
    session_of,
):
    first_flipped_kernel, second_flipped_kernel = (
        lax.all_to_all(first_kernel, "section", split_axis=1, concat_axis=2, tiled=True),
        lax.all_to_all(second_kernel, "section", split_axis=1, concat_axis=2, tiled=True),
    )
    upstream_gradient = layer_backprop(
        output_gradient, second_preactivation, second_flipped_kernel, SECOND_DILATION
    )
    input_gradient = layer_backprop(
        upstream_gradient, first_preactivation, first_flipped_kernel, FIRST_DILATION
    )
    trial_shards = lax.axis_size("trial")
    neurons, trials, steps_count = spike_rates.shape
    neuron_blocks = spike_rates.reshape(trial_shards, neurons // trial_shards, trials, steps_count)
    partials = jnp.einsum(
        "jbil,cil->jibc", neuron_blocks, input_gradient, preferred_element_type=jnp.float32
    )
    arrived = lax.all_to_all(
        partials.astype(jnp.bfloat16), "trial", split_axis=0, concat_axis=0, tiled=True
    ).astype(partials.dtype)
    every_id = lax.all_gather(session_of, "trial", axis=0, tiled=True)
    total_trials = every_id.shape[0]
    flat_parts = arrived.reshape(total_trials, -1)
    session_list = jnp.arange(trial_shards, dtype=jnp.int32)
    first_trial = jnp.sum((every_id[None, :] < session_list[:, None]).astype(jnp.int32), axis=1)

    def add_offset(offset, running):
        position = first_trial + offset
        clipped = jnp.minimum(position, total_trials - 1)
        rows_here = jnp.take(flat_parts, clipped, axis=0)
        valid = (position < total_trials) & (jnp.take(every_id, clipped, axis=0) == session_list)
        return running + jnp.where(valid[:, None], rows_here, 0.0)

    start_sums = jnp.zeros((trial_shards, flat_parts.shape[1]), jnp.float32)
    summed = lax.fori_loop(0, MOST, add_offset, start_sums)
    return summed.reshape(trial_shards, neurons // trial_shards, input_gradient.shape[0]).astype(
        jnp.bfloat16
    )


def solution(mesh):
    in_specs = (
        P(None, "trial", None),
        P("section", "trial", None),
        P("section", "trial", None),
        P("section", "trial", None),
        P(None, None, "section"),
        P(None, None, "section"),
        P("trial"),
    )
    out_specs = P(None, "trial", "section")
    return jax.shard_map(body, mesh=mesh, in_specs=in_specs, out_specs=out_specs, check_vma=False)
```

profile of v0, /device:TPU:8, one launch (start us, length us, event | category | flops | bytes accessed | tf_op | source)
XLA Modules:
  0.0 186.1 jit_solution(364001516441620479)
XLA Ops:
  6.5 1.2 copy.50
  7.8 1.1 copy.51
  8.9 1.0 fusion.14
  9.9 2.7 %copy.52 = bf16[3,1024,256]{2,0,1:T(4,128)(2,1)} copy(bf16[3,1024,256]{2,1,0:T(8,128)(2,1)S(1)} %copy-done.3) | data formatting | bytes 3145728 | tf_op args[5]
  12.6 4.4 %all-to-all-start = ((bf16[3,1024,256]{2,0,1:T(4,128)(2,1)}), bf16[3,1024,256]{2,0,1:T(4,128)(2,1)S(1)}, u32[]{:S(2)}, u32[]{:S(2)}) async-start(bf16[3,1024,256]{2,0,1:T(4,128)(2,1)} %copy.52), calls=%async_computation | async-start | bytes 4194304 | tf_op jit(solution)/shard_map/all_to_all | solution.py:56
  17.2 29.0 %all-to-all-done = bf16[3,1024,256]{2,0,1:T(4,128)(2,1)S(1)} async-done(((bf16[3,1024,256]{2,0,1:T(4,128)(2,1)}), bf16[3,1024,256]{2,0,1:T(4,128)(2,1)S(1)}, u32[]{:S(2)}, u32[]{:S(2)}) %all-to-all-start) | async-done | bytes 1572896 | tf_op jit(solution)/shard_map/all_to_all | solution.py:56
  46.2 1.5 copy.79
  49.4 6.2 %all-gather.3.cloned.1.call-done = bf16[1024,2,256]{0,2,1:T(8,128)(2,1)} async-done(((bf16[256,2,256]{0,2,1:T(8,128)(2,1)}), bf16[1024,2,256]{0,2,1:T(8,128)(2,1)}) %all-gather.3.cloned.1.call-update) | async-done | bytes 1048592 | tf_op jit(solution)/shard_map/all_gather | solution.py:41
  55.6 1.8 convolution_bitcast_fusion.4
  57.9 1.5 fusion.31
  59.4 1.4 copy.55
  60.8 31.6 %all_to_all.35 = bf16[3,1024,256]{2,0,1:T(4,128)(2,1)S(1)} all-to-all(bf16[3,1024,256]{2,0,1:T(4,128)(2,1)S(1)} %copy.55), channel_id=1, replica_groups=mesh['section'=4,'trial'=128] {'section'}, dimensions={1} | all-to-all | bytes 3145728 | tf_op jit(solution)/shard_map/all_to_all | solution.py:55
  93.3 7.2 %all-gather.5.cloned.1.call-done = bf16[1024,2,256]{0,2,1:T(8,128)(2,1)} async-done(((bf16[256,2,256]{0,2,1:T(8,128)(2,1)}), bf16[1024,2,256]{0,2,1:T(8,128)(2,1)}) %all-gather.5.cloned.1.call-update) | async-done | bytes 1048592 | tf_op jit(solution)/shard_map/all_gather | solution.py:41
  100.5 1.8 convolution_bitcast_fusion.1
  102.8 2.0 %fusion.3 = bf16[128,2,4,256]{0,3,2,1:T(8,128)(2,1)S(1)} fusion(f32[256,2,256]{0,2,1:T(8,128)} %get-tuple-element.154, bf16[1024,2,256]{0,2,1:T(8,128)(2,1)S(1)} %copy-done.1, bf16[256,1024,1]{0,1,2:T(8,128)(2,1)S(1)} %bitcast.90, bf16[128,4,2,256]{3,2,1,0:T(2,128)(2,1)S(1)} %bitcast.84, f32[256,2,192]{0,2,1:T(8,128)S(1)} %slice.59, ...), kind=kOutput, calls=%fused_computation.13 | convolution fusion | flops 403439616 | bytes 3997696 | tf_op jit(solution)/shard_map/jbil,cil->jibc/dot_general | solution.py:67
  104.8 1.2 copy.65
  106.0 19.0 %all-to-all-start.2 = ((bf16[128,2,4,256]{3,2,1,0:T(4,128)(2,1)}), bf16[128,2,4,256]{3,2,1,0:T(4,128)(2,1)S(1)}, u32[]{:S(2)}, u32[]{:S(2)}) async-start(bf16[128,2,4,256]{3,2,1,0:T(4,128)(2,1)} %copy.65), calls=%async_computation.2 | async-start | bytes 1048576 | tf_op jit(solution)/shard_map/all_to_all | solution.py:70
  125.0 1.2 dynamic-slice
  127.1 37.2 %all-reduce.4 = s32[256]{0:T(256)S(1)} all-reduce(s32[256]{0:T(256)S(1)} %dynamic-update-slice), channel_id=1, replica_groups=mesh['section'=4,'trial'=128] {'trial'}, use_global_device_ids=true, to_apply=%add.4 | all-reduce | flops 256 | bytes 2048
  164.5 13.8 %while.14 = (s32[]{:T(128)}, f32[128,1024]{1,0:T(8,128)S(1)}, s32[128]{0:T(128)S(1)}, s32[256]{0:T(256)S(1)}, f32[256,1024]{1,0:T(8,128)S(1)}, /*index=5*/s32[]{:T(128)}, s32[]{:T(128)}) while((s32[]{:T(128)}, f32[128,1024]{1,0:T(8,128)S(1)}, s32[128]{0:T(128)S(1)}, s32[256]{0:T(256)S(1)}, f32[256,1024]{1,0:T(8,128)S(1)}, ...), condition=%wide.region_2.3_spmd.clone, body=%wide.region_1.2_spmd.clone.sunk | while | flops 527491 | bytes 2630751 | solution.py:87
  164.6 1.3 gather_fusion.1
  165.9 0.8 gather_fusion
  166.9 1.3 gather_fusion.1
  168.1 0.8 gather_fusion
  169.2 1.3 gather_fusion.1
  170.4 0.8 gather_fusion
  171.5 1.3 gather_fusion.1
  172.7 0.8 gather_fusion
  173.7 1.3 gather_fusion.1
  175.0 0.8 gather_fusion
  176.0 1.3 gather_fusion.1
  178.3 0.9 convert_element_type.61
  (66 shorter events, 6.2 us)
Async XLA Ops:
  6.5 96.3 %copy-start = (bf16[512,2,256]{2,1,0:T(2,128)(2,1)S(1)}, bf16[512,2,256]{2,1,0:T(2,128)(2,1)}, u32[]{:S(2)}) copy-start(bf16[512,2,256]{2,1,0:T(2,128)(2,1)} %param.9) | copy-start | bytes 1572868
  6.5 3.4 %copy-start.3 = (bf16[3,1024,256]{2,1,0:T(8,128)(2,1)S(1)}, bf16[3,1024,256]{2,1,0:T(8,128)(2,1)}, u32[]{:S(2)}) copy-start(bf16[3,1024,256]{2,1,0:T(8,128)(2,1)} %param.14) | copy-start | bytes 4718596
  6.5 49.0 %all-gather.3.cloned.1.call-start = ((), (), s32[]{:S(2)}) async-start(), calls=%async_computation.3 | async-start | bytes 1310720 | tf_op jit(solution)/shard_map/all_gather | solution.py:41
  12.6 4.4 %copy-start.5 = (bf16[256,2,256]{2,1,0:T(2,128)(2,1)S(1)}, bf16[256,2,256]{2,1,0:T(2,128)(2,1)}, u32[]{:S(2)}) copy-start(bf16[256,2,256]{2,1,0:T(2,128)(2,1)} %param.10) | copy-start | bytes 786436
  12.6 33.6 %all-to-all-start = ((bf16[3,1024,256]{2,0,1:T(4,128)(2,1)}), bf16[3,1024,256]{2,0,1:T(4,128)(2,1)S(1)}, u32[]{:S(2)}, u32[]{:S(2)}) async-start(bf16[3,1024,256]{2,0,1:T(4,128)(2,1)} %copy.52), calls=%async_computation | async-start | bytes 4194304 | tf_op jit(solution)/shard_map/all_to_all | solution.py:56
  17.0 83.5 %all-gather.5.cloned.1.call-start = ((), (), s32[]{:S(2)}) async-start(), calls=%async_computation.4 | async-start | bytes 1310720 | tf_op jit(solution)/shard_map/all_gather | solution.py:41
  55.6 1.8 copy-start.2
  57.9 1.5 copy-start.4
  100.5 1.8 copy-start.1
  104.8 22.1 %copy-start.6 = (s32[2]{0:T(128)S(1)}, s32[2]{0:T(128)}, u32[]{:S(2)}) copy-start(s32[2]{0:T(128)} %param.15) | copy-start | bytes 28
  106.0 58.4 %all-to-all-start.2 = ((bf16[128,2,4,256]{3,2,1,0:T(4,128)(2,1)}), bf16[128,2,4,256]{3,2,1,0:T(4,128)(2,1)S(1)}, u32[]{:S(2)}, u32[]{:S(2)}) async-start(bf16[128,2,4,256]{3,2,1,0:T(4,128)(2,1)} %copy.65), calls=%async_computation.2 | async-start | bytes 1048576 | tf_op jit(solution)/shard_map/all_to_all | solution.py:70
Sparse Core Ops, SparseCore 0:
  10.0 45.5 all-gather.2
  59.5 40.9 all-gather.4
where the time goes:
time: 187 us; the launch traced here: 186 us
  blocking collectives  68.8 us (37%)
  waiting for transfers between devices  42.5 us (23%)
  local copies, waits for them, and re-layouts  26.8 us (14%)
  starting transfers between devices  23.4 us (13%)
  between operations  14.2 us (8%)
  matrix products  7.88 us (4%)
  other arithmetic  2.14 us (1%)
    unnamed x1, blocking collectives  37.2 us
    all_to_all x1, blocking collectives, body(): lax.all_to_all(first_kernel, 'section', split_axis=1, concat_axis=2, tile...  31.6 us
    all_to_all x1, waiting for transfers between devices, body(): lax.all_to_all(second_kernel, 'section', split_axis=1, concat_axis=2, til...  29 us
    all_to_all x1, starting transfers between devices, body(): lax.all_to_all(partials.astype(jnp.bfloat16), 'trial', split_axis=0, conc...  19 us
    all_gather x2, waiting for transfers between devices, layer_backprop(): lax.all_gather(flow_grad, 'section', axis=0, tiled=True)  13.4 us
    unnamed x23, local copies, waits for them, and re-layouts  8.19 us
    gather x6, local copies, waits for them, and re-layouts, add_offset(): jnp.take(every_id, clipped, axis=0) == session_list  7.59 us
    dot_general x5, matrix products, tap_sum(): lax.dot_general(weights[kernel_tap], flow_grad, (((1,), (0,)), ((), ())),...  5.91 us
  transfers between devices with their start and end apart: 4, of which 3 were waited for; matrix products, arithmetic and copies ran while one was open for 5% of the time, Pallas kernels for 0%

commit v1 on v0

--- a/solution.py
+++ b/solution.py
@@ -38,7 +38,14 @@
 
 def layer_backprop(upstream, preact, turned, spacing):
     flow_grad = (upstream.astype(jnp.float32) * gelu_slope(preact)).astype(jnp.bfloat16)
-    back_sum = tap_sum(turned, lax.all_gather(flow_grad, "section", axis=0, tiled=True), spacing)
+    back_sum = tap_sum(
+        turned,
+        jnp.concatenate(
+            lax.all_to_all(jnp.stack([flow_grad] * lax.axis_size("section")), "section", 0, 0),
+            axis=0,
+        ),
+        spacing,
+    )
     return (upstream.astype(jnp.float32) + back_sum).astype(jnp.bfloat16)
 
 

time: 187 us -> 180 us (0.963)
  blocking collectives: 68.8 us -> 37.1 us
  local copies, waits for them, and re-layouts: 26.8 us -> 43.6 us
  between operations: 14.2 us -> 0.95 us
  starting transfers between devices: 23.4 us -> 35.6 us
  waiting for transfers between devices: 42.5 us -> 52.1 us
    all_to_all x1 -> x0, blocking collectives: 31.6 us -> none  [body(): lax.all_to_all(first_kernel, 'section', split_axis=1, concat_axis=2, tile...]
    all_to_all x0 -> x3, waiting for transfers between devices: none -> 30.8 us  [the longest x2 19 us: layer_backprop(): lax.all_to_all(jnp.stack([flow_grad] * lax.axis_size('section')), 'sectio...]
    all_gather x2 -> x0, waiting for transfers between devices: 13.4 us -> none  [layer_backprop(): lax.all_gather(flow_grad, 'section', axis=0, tiled=True)]
    all_to_all x0 -> x3, starting transfers between devices: none -> 12.4 us  [the longest x2 7.99 us: layer_backprop(): lax.all_to_all(jnp.stack([flow_grad] * lax.axis_size('section')), 'sectio...]
    unnamed x23 -> x25, local copies, waits for them, and re-layouts: 8.19 us -> 16.5 us
    all_to_all x1, waiting for transfers between devices: 29 us -> 21.3 us  [body(): lax.all_to_all(second_kernel, 'section', split_axis=1, concat_axis=2, til...]
    another operation x0 -> x2, local copies, waits for them, and re-layouts: none -> 2.09 us  [layer_backprop(): jnp.stack([flow_grad] * lax.axis_size('section'))]
  transfers between devices with their start and end apart: 4 -> 5, of which waited for: 3 -> 4; matrix products, arithmetic and copies ran while one was open for 5% -> 14% of each run, Pallas kernels for 0% -> 0%
where the time goes in v1:
time: 180 us; the launch traced here: 179 us
  waiting for transfers between devices  52.1 us (29%)
  local copies, waits for them, and re-layouts  43.6 us (24%)
  blocking collectives  37.1 us (21%)
  starting transfers between devices  35.6 us (20%)
  matrix products  8.35 us (5%)
    unnamed x1, blocking collectives  37.1 us
    all_to_all x1, waiting for transfers between devices, body(): lax.all_to_all(second_kernel, 'section', split_axis=1, concat_axis=2, til...  21.3 us
    all_to_all x1, starting transfers between devices, body(): lax.all_to_all(partials.astype(jnp.bfloat16), 'trial', split_axis=0, conc...  19.5 us
    all_to_all x2, waiting for transfers between devices, layer_backprop(): lax.all_to_all(jnp.stack([flow_grad] * lax.axis_size('section')), 'sectio...  19 us
    unnamed x25, local copies, waits for them, and re-layouts  16.5 us
    all_to_all x1, waiting for transfers between devices, body(): lax.all_to_all(first_kernel, 'section', split_axis=1, concat_axis=2, tile...  11.9 us
    all_to_all x2, starting transfers between devices, layer_backprop(): lax.all_to_all(jnp.stack([flow_grad] * lax.axis_size('section')), 'sectio...  7.99 us
    gather x6, local copies, waits for them, and re-layouts, add_offset(): jnp.take(every_id, clipped, axis=0) == session_list  7.59 us
  transfers between devices with their start and end apart: 5, of which 4 were waited for; matrix products, arithmetic and copies ran while one was open for 14% of the time, Pallas kernels for 0%

profile of v1, /device:TPU:8, one launch (start us, length us, event | category | flops | bytes accessed | tf_op | source)
XLA Modules:
  0.0 179.4 jit_solution(3173039155457711647)
XLA Ops:
  0.0 1.2 copy.54
  1.2 1.1 copy.55
  3.6 4.3 %all-to-all-start = ((bf16[4,256,2,256]{1,3,2,0:T(8,128)(2,1)}), bf16[4,256,2,256]{1,3,2,0:T(8,128)(2,1)S(1)}, u32[]{:S(2)}, u32[]{:S(2)}) async-start(bf16[4,256,2,256]{1,3,2,0:T(8,128)(2,1)} %stack.4), calls=%async_computation | async-start | bytes 2097152 | tf_op jit(solution)/shard_map/all_to_all | solution.py:44
  7.9 4.1 %copy.57 = bf16[3,1024,256]{2,0,1:T(4,128)(2,1)} copy(bf16[3,1024,256]{2,1,0:T(8,128)(2,1)} %param.14) | data formatting | bytes 3145728 | tf_op args[5]
  12.0 11.0 %all-to-all-done = bf16[4,256,2,256]{1,3,2,0:T(8,128)(2,1)S(1)} async-done(((bf16[4,256,2,256]{1,3,2,0:T(8,128)(2,1)}), bf16[4,256,2,256]{1,3,2,0:T(8,128)(2,1)S(1)}, u32[]{:S(2)}, u32[]{:S(2)}) %all-to-all-start) | async-done | bytes 1048608 | tf_op jit(solution)/shard_map/all_to_all | solution.py:44
  24.0 3.6 %all-to-all-start.1 = ((bf16[3,1024,256]{2,0,1:T(4,128)(2,1)}), bf16[3,1024,256]{2,0,1:T(4,128)(2,1)S(1)}, u32[]{:S(2)}, u32[]{:S(2)}) async-start(bf16[3,1024,256]{2,0,1:T(4,128)(2,1)} %copy.57), calls=%async_computation.1 | async-start | bytes 4194304 | tf_op jit(solution)/shard_map/all_to_all | solution.py:63
  27.6 4.1 %copy.61 = bf16[3,1024,256]{2,0,1:T(4,128)(2,1)} copy(bf16[3,1024,256]{2,1,0:T(8,128)(2,1)} %param.13) | data formatting | bytes 3145728 | tf_op args[4]
  31.7 21.3 %all-to-all-done.1 = bf16[3,1024,256]{2,0,1:T(4,128)(2,1)S(1)} async-done(((bf16[3,1024,256]{2,0,1:T(4,128)(2,1)}), bf16[3,1024,256]{2,0,1:T(4,128)(2,1)S(1)}, u32[]{:S(2)}, u32[]{:S(2)}) %all-to-all-start.1) | async-done | bytes 1572896 | tf_op jit(solution)/shard_map/all_to_all | solution.py:63
  53.0 1.4 copy-done.1
  54.3 4.4 %all-to-all-start.3 = ((bf16[3,1024,256]{2,0,1:T(4,128)(2,1)}), bf16[3,1024,256]{2,0,1:T(4,128)(2,1)}, u32[]{:S(2)}, u32[]{:S(2)}) async-start(bf16[3,1024,256]{2,0,1:T(4,128)(2,1)} %copy.61), calls=%async_computation.3 | async-start | bytes 4194304 | tf_op jit(solution)/shard_map/all_to_all | solution.py:62
  59.7 1.5 copy.81
  61.6 1.5 copy.87
  63.6 1.2 reshape.117
  64.8 1.5 convolution_bitcast_fusion.4
  69.1 2.4 %fusion.31 = (bf16[256,2,256]{0,2,1:T(8,128)(2,1)S(1)}, f32[256,2,256]{0,2,1:T(8,128)}) fusion(bf16[256,2,256]{0,2,1:T(8,128)(2,1)} %copy.59, f32[256,2,128]{0,2,1:T(8,128)} %slice.54, f32[256,2,192]{0,2,1:T(8,128)S(1)} %slice-done, bf16[1024,2,256]{0,2,1:T(8,128)(2,1)S(1)} %bitcast.95, bf16[256,1024,1]{1,0,2:T(8,128)(2,1)S(1)} %reshape.116, ...), kind=kOutput, calls=%fused_computation.56 | convolution fusion | flops 270663680 | bytes 3538944 | tf_op jit(solution)/shard_map/dot_general | solution.py:27
  71.5 11.9 %all-to-all-done.3 = bf16[3,1024,256]{2,0,1:T(4,128)(2,1)} async-done(((bf16[3,1024,256]{2,0,1:T(4,128)(2,1)}), bf16[3,1024,256]{2,0,1:T(4,128)(2,1)}, u32[]{:S(2)}, u32[]{:S(2)}) %all-to-all-start.3) | async-done | bytes 1572896 | tf_op jit(solution)/shard_map/all_to_all | solution.py:62
  84.4 3.7 %all-to-all-start.2 = ((bf16[4,256,2,256]{1,3,2,0:T(8,128)(2,1)}), bf16[4,256,2,256]{1,3,2,0:T(8,128)(2,1)S(1)}, u32[]{:S(2)}, u32[]{:S(2)}) async-start(bf16[4,256,2,256]{1,3,2,0:T(8,128)(2,1)} %stack.5), calls=%async_computation.2 | async-start | bytes 2097152 | tf_op jit(solution)/shard_map/all_to_all | solution.py:44
  88.1 1.8 %copy.62 = bf16[3,1024,256]{2,1,0:T(8,128)(2,1)S(1)} copy(bf16[3,1024,256]{2,0,1:T(4,128)(2,1)} %all-to-all-done.3) | data formatting | bytes 3145728 | tf_op jit(solution)/shard_map/all_to_all | solution.py:62
  92.3 7.9 %all-to-all-done.2 = bf16[4,256,2,256]{1,3,2,0:T(8,128)(2,1)S(1)} async-done(((bf16[4,256,2,256]{1,3,2,0:T(8,128)(2,1)}), bf16[4,256,2,256]{1,3,2,0:T(8,128)(2,1)S(1)}, u32[]{:S(2)}, u32[]{:S(2)}) %all-to-all-start.2) | async-done | bytes 1048608 | tf_op jit(solution)/shard_map/all_to_all | solution.py:44
  100.3 1.5 convolution_bitcast_fusion.1
  102.5 2.0 %fusion.3 = bf16[128,2,4,256]{0,3,2,1:T(8,128)(2,1)S(1)} fusion(f32[256,2,256]{0,2,1:T(8,128)} %get-tuple-element.154, bf16[1024,2,256]{0,2,1:T(8,128)(2,1)S(1)} %bitcast.92, bf16[256,1024,1]{0,1,2:T(8,128)(2,1)S(1)} %bitcast.102, bf16[128,4,2,256]{3,2,1,0:T(2,128)(2,1)S(1)} %bitcast.88, f32[256,2,192]{0,2,1:T(8,128)S(1)} %slice.59, ...), kind=kOutput, calls=%fused_computation.13 | convolution fusion | flops 403439616 | bytes 3997696 | tf_op jit(solution)/shard_map/jbil,cil->jibc/dot_general | solution.py:74
  104.4 1.2 copy.71
  105.6 19.5 %all-to-all-start.4 = ((bf16[128,2,4,256]{3,2,1,0:T(4,128)(2,1)}), bf16[128,2,4,256]{3,2,1,0:T(4,128)(2,1)S(1)}, u32[]{:S(2)}, u32[]{:S(2)}) async-start(bf16[128,2,4,256]{3,2,1,0:T(4,128)(2,1)} %copy.71), calls=%async_computation.4 | async-start | bytes 1048576 | tf_op jit(solution)/shard_map/all_to_all | solution.py:77
  125.2 1.3 dynamic-slice
  127.4 37.1 %all-reduce.4 = s32[256]{0:T(256)S(1)} all-reduce(s32[256]{0:T(256)S(1)} %dynamic-update-slice), channel_id=1, replica_groups=mesh['section'=4,'trial'=128] {'trial'}, use_global_device_ids=true, to_apply=%add.4 | all-reduce | flops 256 | bytes 2048
  164.7 13.8 %while.14 = (s32[]{:T(128)}, f32[128,1024]{1,0:T(8,128)S(1)}, s32[128]{0:T(128)S(1)}, s32[256]{0:T(256)S(1)}, f32[256,1024]{1,0:T(8,128)S(1)}, /*index=5*/s32[]{:T(128)}, s32[]{:T(128)}) while((s32[]{:T(128)}, f32[128,1024]{1,0:T(8,128)S(1)}, s32[128]{0:T(128)S(1)}, s32[256]{0:T(256)S(1)}, f32[256,1024]{1,0:T(8,128)S(1)}, ...), condition=%wide.region_2.3_spmd.clone, body=%wide.region_1.2_spmd.clone.sunk | while | flops 527491 | bytes 2630751 | solution.py:94
  164.7 1.3 gather_fusion.1
  167.0 1.3 gather_fusion.1
  169.3 1.3 gather_fusion.1
  171.6 1.3 gather_fusion.1
  173.9 1.3 gather_fusion.1
  176.2 1.3 gather_fusion.1
  (72 shorter events, 18.1 us)
Async XLA Ops:
  0.0 102.4 %copy-start = (bf16[512,2,256]{2,1,0:T(2,128)(2,1)S(1)}, bf16[512,2,256]{2,1,0:T(2,128)(2,1)}, u32[]{:S(2)}) copy-start(bf16[512,2,256]{2,1,0:T(2,128)(2,1)} %param.9) | copy-start | bytes 1572868
  3.6 19.4 %all-to-all-start = ((bf16[4,256,2,256]{1,3,2,0:T(8,128)(2,1)}), bf16[4,256,2,256]{1,3,2,0:T(8,128)(2,1)S(1)}, u32[]{:S(2)}, u32[]{:S(2)}) async-start(bf16[4,256,2,256]{1,3,2,0:T(8,128)(2,1)} %stack.4), calls=%async_computation | async-start | bytes 2097152 | tf_op jit(solution)/shard_map/all_to_all | solution.py:44
  23.0 1.0 copy-start.3
  24.0 29.0 %all-to-all-start.1 = ((bf16[3,1024,256]{2,0,1:T(4,128)(2,1)}), bf16[3,1024,256]{2,0,1:T(4,128)(2,1)S(1)}, u32[]{:S(2)}, u32[]{:S(2)}) async-start(bf16[3,1024,256]{2,0,1:T(4,128)(2,1)} %copy.57), calls=%async_computation.1 | async-start | bytes 4194304 | tf_op jit(solution)/shard_map/all_to_all | solution.py:63
  31.7 27.1 %copy-start.6 = (bf16[256,2,256]{2,1,0:T(2,128)(2,1)S(1)}, bf16[256,2,256]{2,1,0:T(2,128)(2,1)}, u32[]{:S(2)}) copy-start(bf16[256,2,256]{2,1,0:T(2,128)(2,1)} %param.10) | copy-start | bytes 786436
  53.0 1.4 copy-start.1
  54.3 29.0 %all-to-all-start.3 = ((bf16[3,1024,256]{2,0,1:T(4,128)(2,1)}), bf16[3,1024,256]{2,0,1:T(4,128)(2,1)}, u32[]{:S(2)}, u32[]{:S(2)}) async-start(bf16[3,1024,256]{2,0,1:T(4,128)(2,1)} %copy.61), calls=%async_computation.3 | async-start | bytes 4194304 | tf_op jit(solution)/shard_map/all_to_all | solution.py:62
  59.7 1.9 %copy-start.2 = (bf16[3,1024,256]{2,0,1:T(4,128)(2,1)S(1)}, bf16[3,1024,256]{2,0,1:T(4,128)(2,1)}, u32[]{:S(2)}) copy-start(bf16[3,1024,256]{2,0,1:T(4,128)(2,1)} %copy-done.1) | copy-start | bytes 4718596
  66.3 0.8 copy-start.5
  67.5 1.6 slice-start
  84.4 15.8 %all-to-all-start.2 = ((bf16[4,256,2,256]{1,3,2,0:T(8,128)(2,1)}), bf16[4,256,2,256]{1,3,2,0:T(8,128)(2,1)S(1)}, u32[]{:S(2)}, u32[]{:S(2)}) async-start(bf16[4,256,2,256]{1,3,2,0:T(8,128)(2,1)} %stack.5), calls=%async_computation.2 | async-start | bytes 2097152 | tf_op jit(solution)/shard_map/all_to_all | solution.py:44
  100.3 1.6 copy-start.4
  104.4 22.7 %copy-start.7 = (s32[2]{0:T(128)S(1)}, s32[2]{0:T(128)}, u32[]{:S(2)}) copy-start(s32[2]{0:T(128)} %param.15) | copy-start | bytes 28
  105.6 58.9 %all-to-all-start.4 = ((bf16[128,2,4,256]{3,2,1,0:T(4,128)(2,1)}), bf16[128,2,4,256]{3,2,1,0:T(4,128)(2,1)S(1)}, u32[]{:S(2)}, u32[]{:S(2)}) async-start(bf16[128,2,4,256]{3,2,1,0:T(4,128)(2,1)} %copy.71), calls=%async_computation.4 | async-start | bytes 1048576 | tf_op jit(solution)/shard_map/all_to_all | solution.py:77
